TPU v7x, 128 devices: a whole 4x4x4 slice. The times are simulated.
128 devices in a mesh: blk: 16 (over y_hi, x, core), kv: 8 (over z, y_lo).
Axes of the slice: x: 4, y: 4 (y_hi: 2, y_lo: 2; y = y_hi * 2 + y_lo), z: 4, core: 2. Of those that a mesh axis runs over, the one named last changes fastest.
Arguments:
- tokens: bfloat16 [8192, 2560], P('blk'), may hold values from -6 to 6
- attn_gain: float32 [2560], replicated, may hold values from 0.1 to 1.9
- mlp_gain: float32 [2560], replicated, may hold values from 0.1 to 1.9
- w_query: float32 [2560, 2560], P(('blk', 'kv')), may hold values from -0.375 to 0.375
- w_key: float32 [2560, 640], P(('blk', 'kv')), may hold values from -0.125 to 0.125
- w_value: float32 [2560, 640], P(('blk', 'kv')), may hold values from -0.125 to 0.125
- w_gate: float32 [2560, 6912], P(('blk', 'kv')), may hold values from -0.125 to 0.125
- w_up: float32 [2560, 6912], P(('blk', 'kv')), may hold values from -0.125 to 0.125
- w_out: bfloat16 [2560, 2560], P('kv'), may hold values from -0.125 to 0.125
- w_down: bfloat16 [6912, 2560], P('kv'), may hold values from -0.078125 to 0.078125
- cache: bfloat16 [2, 128, 8, 80, 128], P(None, 'blk', 'kv'), may hold values from -300 to 300
- slot_prompt: int32 [128], replicated, may hold values from 0 to 15, as said below
- prefix_len: int32 [16], replicated, may hold values from 1 to 4096, as said below
- new_len: int32 [16], replicated, may hold values from 256 to 512, as said below
Outputs:
- mixed: bfloat16 [8192, 2560], P('blk', 'kv')
Inputs may be any that keep to these rules, and one draw needn't show every extreme that they name: `slot_prompt`: the 8 slots of one index of blk hold at most 2 blocks of one prompt. One prompt, drawn afresh, has exactly 2 blocks on every index of blk; the other 6 slots of an index hold blocks of distinct prompts; every prompt has at least one block. `prefix_len`: A prompt with c slots has a prefix longer than (c - 1) * 128 and at most c * 128. Rows i >= new_len[p] of prompt p are padding.
All inputs are finite; a program needn't handle non-finite values.
Results may differ from a plain program's by a relative error of at most 0.019.
The roundings to bfloat16 on the way count: a program that leaves them out, or rounds other values in their place, can miss the bound.
Values may be sent and summed in bfloat16 or wider, within the bound.
A program may use at most 128 MiB of HBM per device.

v0:
```python
import math
import jax
import jax.numpy as jnp
from jax import lax
from jax.sharding import PartitionSpec as P

HEADS = 32
KV_HEADS = 8
HD = 80
WINDOW = 4096
SINKS = 4
BLOCK = 128
CAP = 2
FLOOR_SCORE = -1e30
EPSILON = 1e-05
ROPE_BASE = 10000.0


def rms_scale(row_data, gain_vec):
    values = row_data.astype(jnp.float32)
    mean_square = jnp.mean(values * values, axis=-1, keepdims=True)
    return (values * lax.rsqrt(mean_square + EPSILON) * gain_vec).astype(jnp.bfloat16)


def rotate(values, positions):
    head_width = values.shape[-1]
    half_width = head_width // 2
    frequency = ROPE_BASE ** (-2.0 * jnp.arange(half_width, dtype=jnp.float32) / head_width)
    angles = positions.astype(jnp.float32)[:, None] * frequency[None, :]
    cosine = jnp.cos(angles)[:, None, :]
    sine_wave = jnp.sin(angles)[:, None, :]
    first_half = values[..., :half_width]
    second_half = values[..., half_width:]
    return jnp.concatenate(
        [
            first_half * cosine - second_half * sine_wave,
            second_half * cosine + first_half * sine_wave,
        ],
        axis=-1,
    )


def slot_ranks(slot_prompt, prompts, slots):
    onehot = (slot_prompt[:, None] == jnp.arange(prompts, dtype=jnp.int32)[None, :]).astype(
        jnp.int32
    )
    running = jnp.cumsum(onehot, axis=0)
    global_rank = jnp.sum(onehot * (running - 1), axis=1)
    local_count = jnp.cumsum(onehot.reshape(-1, slots, prompts), axis=1).reshape(-1, prompts)
    local_rank = jnp.sum(onehot * (local_count - 1), axis=1)
    return (global_rank, local_rank)


def visible(query_pos, key_pos):
    distance = query_pos - key_pos
    return (distance >= 0) & ((distance < WINDOW) | (key_pos < SINKS))


def partial_block(scores, seen_mask):
    masked = jnp.where(seen_mask, scores, FLOOR_SCORE)
    row_max = jnp.max(masked, axis=-1)
    weights = jnp.where(seen_mask, jnp.exp(masked - row_max[..., None]), 0.0)
    return (row_max, jnp.sum(weights, axis=-1), weights.astype(jnp.bfloat16))


def combine(first_part, second_part):
    maxima = jnp.maximum(first_part[0], second_part[0])
    scale_first = jnp.exp(first_part[0] - maxima)
    scale_second = jnp.exp(second_part[0] - maxima)
    totals = first_part[1] * scale_first + second_part[1] * scale_second
    outputs = first_part[2] * scale_first[..., None] + second_part[2] * scale_second[..., None]
    return (maxima, totals, outputs)


def pack_groups(matrices, groups):
    pieces = [
        matrix.reshape(matrix.shape[0], groups, matrix.shape[1] // groups) for matrix in matrices
    ]
    joined = jnp.concatenate(pieces, axis=2)
    return joined.reshape(matrices[0].shape[0], -1).astype(jnp.bfloat16)


def restack(moved_rows, groups, n_blocks):
    columns = moved_rows.shape[1]
    ordered = moved_rows.reshape(groups, n_blocks, -1, columns)
    return jnp.transpose(ordered, (1, 0, 2, 3)).reshape(-1, columns)


def shards(
    tokens,
    attn_gain,
    mlp_gain,
    w_query,
    w_key,
    w_value,
    w_gate,
    w_up,
    w_out,
    w_down,
    cache,
    slot_prompt,
    prefix_len,
    new_len,
):
    groups = lax.axis_size("kv")
    n_blocks = lax.axis_size("blk")
    blk_index = lax.axis_index("blk")
    kv_index = lax.axis_index("kv")
    merged_attn = pack_groups((w_query, w_key, w_value), groups)
    merged_mlp = pack_groups((w_gate, w_up), groups)
    collected = (
        lax.all_gather(merged_attn, "blk", axis=0, tiled=True),
        lax.all_gather(merged_mlp, "blk", axis=0, tiled=True),
    )
    moved_attn, moved_mlp = (
        lax.all_to_all(collected[0], "kv", split_axis=1, concat_axis=0, tiled=True),
        lax.all_to_all(collected[1], "kv", split_axis=1, concat_axis=0, tiled=True),
    )
    w_qkv = restack(moved_attn, groups, n_blocks)
    w_pair = restack(moved_mlp, groups, n_blocks)
    query_width = w_query.shape[1] // groups
    key_width = w_key.shape[1] // groups
    kv_local = key_width // HD
    per_group = HEADS // KV_HEADS
    new_rows = tokens.shape[0]
    prompts = prefix_len.shape[0]
    slots = cache.shape[1]
    score_scale = 1.0 / math.sqrt(HD)
    prefix_here = prefix_len[blk_index]
    live_count = new_len[blk_index]
    row_ids = jnp.arange(new_rows, dtype=jnp.int32)
    positions = prefix_here + row_ids
    offsets = jnp.arange(BLOCK, dtype=jnp.int32)
    normed = rms_scale(tokens, attn_gain)
    projected = jnp.dot(normed, w_qkv, preferred_element_type=jnp.float32)
    queries = rotate(projected[:, :query_width].reshape(new_rows, -1, HD), positions).astype(
        jnp.bfloat16
    )
    key_new = rotate(
        projected[:, query_width : query_width + key_width].reshape(new_rows, kv_local, HD),
        positions,
    ).astype(jnp.bfloat16)
    value_new = (
        projected[:, query_width + key_width :].reshape(new_rows, kv_local, HD).astype(jnp.bfloat16)
    )
    grouped_q = queries.reshape(new_rows, kv_local, per_group, HD)
    own_scores = (
        jnp.einsum("qgnd,kgd->gnqk", grouped_q, key_new, preferred_element_type=jnp.float32)
        * score_scale
    )
    own_mask = (row_ids[None, :] < live_count) & visible(positions[:, None], positions[None, :])
    own_max, own_sum, own_weights = partial_block(own_scores, own_mask)
    own_out = jnp.einsum(
        "gnqk,kgd->gnqd", own_weights, value_new, preferred_element_type=jnp.float32
    )
    running = (own_max, own_sum, own_out)
    global_rank, local_rank = slot_ranks(slot_prompt, prompts, slots)
    own_prompts = lax.dynamic_slice_in_dim(slot_prompt, blk_index * slots, slots)
    own_ranks = lax.dynamic_slice_in_dim(local_rank, blk_index * slots, slots)
    placed = own_prompts * CAP + own_ranks
    buffer_ids = jnp.arange(prompts * CAP, dtype=jnp.int32)
    matches = placed[None, :] == buffer_ids[:, None]
    source_slot = jnp.sum(
        jnp.where(matches, jnp.arange(slots, dtype=jnp.int32)[None, :], 0), axis=1
    )
    filled = jnp.any(matches, axis=1)
    outgoing = jnp.where(
        filled[None, :, None, None, None],
        jnp.take(cache, source_slot, axis=1),
        jnp.zeros((), cache.dtype),
    )
    arrived = lax.all_to_all(outgoing, "blk", split_axis=1, concat_axis=1, tiled=True)
    slot_ids = jnp.arange(prompts * slots, dtype=jnp.int32)
    landing = slot_ids // slots * CAP + local_rank
    for_me = slot_prompt == blk_index
    received = (landing[None, :] == buffer_ids[:, None]) & for_me[None, :]
    block_number = jnp.sum(jnp.where(received, global_rank[None, :], 0), axis=1)
    block_live = jnp.any(received, axis=1)
    total_slots = prompts * CAP
    group_slots = min(total_slots, max(1, 512 // BLOCK))
    step_count = total_slots // group_slots
    key_blocks = arrived[0].reshape(step_count, group_slots, kv_local, HD, BLOCK)
    value_blocks = arrived[1].reshape(step_count, group_slots, kv_local, HD, BLOCK)
    numbers = block_number.reshape(step_count, group_slots)
    live_flags = block_live.reshape(step_count, group_slots)

    def prefix_step(running_state, inputs):
        key_part, value_part, number_part, flag_part = inputs
        scores = (
            jnp.einsum("qgnd,sgdt->gnqst", grouped_q, key_part, preferred_element_type=jnp.float32)
            * score_scale
        )
        scores = scores.reshape(kv_local, per_group, new_rows, group_slots * BLOCK)
        key_pos = number_part[:, None] * BLOCK + offsets[None, :]
        key_live = (flag_part[:, None] & (key_pos < prefix_here)).reshape(-1)
        seen_mask = key_live[None, :] & visible(positions[:, None], key_pos.reshape(-1)[None, :])
        block_max, block_sum, weights = partial_block(scores, seen_mask)
        weights = weights.reshape(kv_local, per_group, new_rows, group_slots, BLOCK)
        block_out = jnp.einsum(
            "gnqst,sgdt->gnqd", weights, value_part, preferred_element_type=jnp.float32
        )
        return (combine(running_state, (block_max, block_sum, block_out)), None)

    running = lax.scan(prefix_step, running, (key_blocks, value_blocks, numbers, live_flags))[0]
    totals = running[1]
    outputs = running[2]
    attended = (
        jnp.transpose(outputs / totals[..., None], (2, 0, 1, 3))
        .reshape(new_rows, -1)
        .astype(jnp.bfloat16)
    )
    projected_out = jnp.dot(attended, w_out, preferred_element_type=jnp.float32)
    summed = lax.psum(projected_out.astype(jnp.bfloat16), "kv").astype(jnp.float32)
    middle = (tokens.astype(jnp.float32) + summed).astype(jnp.bfloat16)
    normed_mid = rms_scale(middle, mlp_gain)
    paired = jnp.dot(normed_mid, w_pair, preferred_element_type=jnp.float32)
    hidden_width = w_pair.shape[1] // 2
    hidden = (jax.nn.silu(paired[:, :hidden_width]) * paired[:, hidden_width:]).astype(jnp.bfloat16)
    down_part = jnp.dot(hidden, w_down, preferred_element_type=jnp.float32)
    reduced = lax.psum_scatter(
        down_part.astype(jnp.bfloat16), "kv", scatter_dimension=1, tiled=True
    ).astype(jnp.float32)
    out_width = reduced.shape[1]
    residual = lax.dynamic_slice_in_dim(middle, kv_index * out_width, out_width, 1).astype(
        jnp.float32
    )
    mixed = jnp.where((row_ids < live_count)[:, None], residual + reduced, 0.0)
    return mixed.astype(jnp.bfloat16)


def solution(mesh):
    return jax.shard_map(
        shards,
        mesh=mesh,
        in_specs=(
            P("blk", None),
            P(),
            P(),
            P(("blk", "kv"), None),
            P(("blk", "kv"), None),
            P(("blk", "kv"), None),
            P(("blk", "kv"), None),
            P(("blk", "kv"), None),
            P("kv", None),
            P("kv", None),
            P(None, "blk", "kv", None, None),
            P(),
            P(),
            P(),
        ),
        out_specs=P("blk", "kv"),
        check_vma=False,
    )
```

profile of v0, /device:TPU:1, one launch (start us, length us, event | category | flops | bytes accessed | tf_op | source)
XLA Modules:
  0.0 535.5 jit_solution(12732997169242167067)
XLA Ops:
  18.9 8.4 %all-to-all-start.1 = ((bf16[2,32,1,80,128]{4,3,0,2,1:T(8,128)(2,1)}), bf16[2,32,1,80,128]{4,3,0,2,1:T(8,128)(2,1)S(1)}, u32[]{:S(2)}, u32[]{:S(2)}) async-start(bf16[2,32,1,80,128]{4,3,0,2,1:T(8,128)(2,1)} %fusion.68), calls=%async_computation.1 | async-start | bytes 2621440 | tf_op jit(solution)/shard_map/all_to_all | solution.py:172
  27.4 41.5 %all-gather.5.cloned.1.call-done = bf16[16,20,3840]{2,1,0:T(8,128)(2,1)} async-done(((bf16[1,20,3840]{2,1,0:T(8,128)(2,1)}), bf16[16,20,3840]{2,1,0:T(8,128)(2,1)}) %all-gather.5.cloned.1.call-update) | async-done | bytes 2457616 | tf_op jit(solution)/shard_map/all_gather | solution.py:112
  68.9 6.6 %all_to_all.27 = bf16[320,8,480]{2,1,0:T(8,128)(2,1)} reshape(bf16[16,20,3840]{2,1,0:T(8,128)(2,1)} %all-gather.5.cloned.1.call-done) | data formatting | bytes 4915200 | tf_op jit(solution)/shard_map/all_to_all | solution.py:116
  75.4 4.2 copy.61
  79.6 4.7 all-to-all-start
  85.6 4.4 copy.60
  97.2 29.5 %all-to-all-done = bf16[320,8,480]{2,0,1:T(8,128)(2,1)} async-done(((bf16[320,8,480]{2,0,1:T(8,128)(2,1)}), bf16[320,8,480]{2,0,1:T(8,128)(2,1)}, u32[]{:S(2)}, u32[]{:S(2)}) %all-to-all-start) | async-done | bytes 2457632 | tf_op jit(solution)/shard_map/all_to_all | solution.py:116
  126.7 3.3 copy.62
  132.9 5.5 %reshape.470 = bf16[2560,480]{1,0:T(8,128)(2,1)} reshape(bf16[16,8,20,480]{3,2,1,0:T(8,128)(2,1)} %copy.63) | data formatting | bytes 4915200 | tf_op jit(solution)/shard_map/reshape | solution.py:86
  138.4 4.2 fusion.55
  146.5 16.6 %all-gather.7.cloned.1.call-done = bf16[16,20,13824]{2,1,0:T(8,128)(2,1)} async-done(((bf16[1,20,13824]{2,1,0:T(8,128)(2,1)}), bf16[16,20,13824]{2,1,0:T(8,128)(2,1)}) %all-gather.7.cloned.1.call-update) | async-done | bytes 8847376 | tf_op jit(solution)/shard_map/all_gather | solution.py:113
  163.1 16.9 %all_to_all.31 = bf16[320,8,1728]{2,1,0:T(8,128)(2,1)} reshape(bf16[16,20,13824]{2,1,0:T(8,128)(2,1)} %all-gather.7.cloned.1.call-done) | data formatting | bytes 17694720 | tf_op jit(solution)/shard_map/all_to_all | solution.py:117
  180.0 8.9 %copy.68 = bf16[320,8,1728]{2,0,1:T(8,128)(2,1)} copy(bf16[320,8,1728]{2,1,0:T(8,128)(2,1)} %all_to_all.31) | data formatting | bytes 17694720 | tf_op jit(solution)/shard_map/all_to_all | solution.py:117
  189.0 5.0 all-to-all-start.2
  194.0 57.9 %while.16 = (s32[]{:T(128)}, f32[1,4,512]{2,1,0:T(4,128)S(1)}, f32[1,4,512]{2,1,0:T(4,128)S(1)}, f32[1,4,512,80]{2,3,1,0:T(8,128)S(1)}, pred[8,4]{1,0:T(8,128)(4...) while((s32[]{:T(128)}, f32[1,4,512]{2,1,0:T(4,128)S(1)}, ...), condition=%wide.region_14.15_spmd.clone.clone, body=%wide.region_11.14_spmd.clone.clone.sunk | while | flops 351253504 | bytes 15599833 | solution.py:204
  252.0 3.1 convolution_convert_fusion.1
  255.3 151.3 %all-reduce.2.cloned.1.call-done = bf16[512,2560]{0,1:T(8,128)(2,1)} async-done(((bf16[512,2560]{0,1:T(8,128)(2,1)}), bf16[512,2560]{0,1:T(8,128)(2,1)}) %all-reduce.2.cloned.1.call-update) | async-done | bytes 2621456 | tf_op jit(solution)/shard_map/psum | solution.py:213
  406.6 5.1 fusion.44
  411.7 12.2 %copy.69 = bf16[320,8,1728]{2,1,0:T(8,128)(2,1)} copy(bf16[320,8,1728]{2,0,1:T(8,128)(2,1)} %all-to-all-done.2) | data formatting | bytes 17694720 | tf_op jit(solution)/shard_map/all_to_all | solution.py:117
  423.9 10.4 %copy.70 = bf16[16,8,20,1728]{3,2,1,0:T(8,128)(2,1)} copy(bf16[16,8,20,1728]{3,1,2,0:T(8,128)(2,1)} %bitcast.203) | data formatting | bytes 17694720 | tf_op jit(solution)/shard_map/transpose | solution.py:86
  434.3 14.4 %reshape.479 = bf16[2560,1728]{1,0:T(8,128)(2,1)} reshape(bf16[16,8,20,1728]{3,2,1,0:T(8,128)(2,1)} %copy.70) | data formatting | bytes 17694720 | tf_op jit(solution)/shard_map/reshape | solution.py:86
  448.6 8.9 %fusion.57 = f32[512,1728]{0,1:T(8,128)S(1)} fusion(bf16[2560,1728]{1,0:T(8,128)(2,1)} %reshape.479, bf16[512,2560]{0,1:T(8,128)(2,1)} %get-tuple-element.184, f32[2560]{0:T(1024)S(1)} %copy-done.4, f32[512]{0:T(512)S(1)} %add_rsqrt_fusion), kind=kOutput, calls=%fused_computation.68 | convolution fusion | flops 4535091200 | bytes 15020032 | tf_op jit(solution)/shard_map/dot_general | solution.py:216
  457.5 7.4 %fusion.51 = bf16[2560,512]{1,0:T(8,128)(2,1)} fusion(bf16[864,2560]{1,0:T(8,128)(2,1)} %param.25, f32[512,1728]{0,1:T(8,128)S(1)} %fusion.57), kind=kOutput, calls=%fused_computation.63 | convolution fusion | flops 2268889088 | bytes 10584064 | tf_op jit(solution)/shard_map/dot_general | solution.py:219
  465.0 61.9 %reduce-scatter.4.cloned.1.call-done = bf16[320,512]{1,0:T(8,128)(2,1)} async-done(((bf16[2560,512]{1,0:T(8,128)(2,1)}), bf16[320,512]{1,0:T(8,128)(2,1)}) %reduce-scatter.4.cloned.1.call-update) | async-done | bytes 327696
  (178 shorter events, 87.0 us)
Async XLA Ops:
  6.5 245.4 %copy-start = (bf16[320,2560]{1,0:T(8,128)(2,1)S(1)}, bf16[320,2560]{1,0:T(8,128)(2,1)}, u32[]{:S(2)}) copy-start(bf16[320,2560]{1,0:T(8,128)(2,1)} %param.24) | copy-start | bytes 4915204
  6.5 9.2 %copy-start.2 = (s32[128]{0:T(128)S(1)}, s32[128]{0:T(128)}, u32[]{:S(2)}) copy-start(s32[128]{0:T(128)} %param.27) | copy-start | bytes 1540
  6.5 62.3 %all-gather.5.cloned.1.call-start = ((), (), s32[]{:S(2)}) async-start(), calls=%async_computation.5 | async-start | bytes 3133440 | tf_op jit(solution)/shard_map/all_gather | solution.py:112
  7.5 9.2 %copy-start.1 = (bf16[2,8,1,80,128]{4,3,2,1,0:T(8,128)(2,1)S(1)}, bf16[2,8,1,80,128]{4,3,2,1,0:T(8,128)(2,1)}, u32[]{:S(2)}) copy-start(bf16[2,8,1,80,128]{4,3,2,1,0:T(8,128)(2,1)} %param.26) | copy-start | bytes 983044
  10.8 152.4 %all-gather.7.cloned.1.call-start = ((), (), s32[]{:S(2)}) async-start(), calls=%async_computation.6 | async-start | bytes 11280384 | tf_op jit(solution)/shard_map/all_gather | solution.py:113
  18.9 60.7 %all-to-all-start.1 = ((bf16[2,32,1,80,128]{4,3,0,2,1:T(8,128)(2,1)}), bf16[2,32,1,80,128]{4,3,0,2,1:T(8,128)(2,1)S(1)}, u32[]{:S(2)}, u32[]{:S(2)}) async-start(bf16[2,32,1,80,128]{4,3,0,2,1:T(8,128)(2,1)} %fusion.68), calls=%async_computation.1 | async-start | bytes 2621440 | tf_op jit(solution)/shard_map/all_to_all | solution.py:172
  75.4 8.9 %copy-start.5 = (s32[16]{0:T(128)S(1)}, s32[16]{0:T(128)}, u32[]{:S(2)}) copy-start(s32[16]{0:T(128)} %param.28) | copy-start | bytes 196
  75.4 9.6 %copy-start.6 = (s32[16]{0:T(128)S(1)}, s32[16]{0:T(128)}, u32[]{:S(2)}) copy-start(s32[16]{0:T(128)} %param.29) | copy-start | bytes 196
  79.6 47.1 %all-to-all-start = ((bf16[320,8,480]{2,0,1:T(8,128)(2,1)}), bf16[320,8,480]{2,0,1:T(8,128)(2,1)}, u32[]{:S(2)}, u32[]{:S(2)}) async-start(bf16[320,8,480]{2,0,1:T(8,128)(2,1)} %copy.61), calls=%async_computation | async-start | bytes 5242880 | tf_op jit(solution)/shard_map/all_to_all | solution.py:116
  132.9 5.5 %copy-start.3 = (f32[2560]{0:T(1024)S(1)}, f32[2560]{0:T(1024)}, u32[]{:S(2)}) copy-start(f32[2560]{0:T(1024)} %param.17) | copy-start | bytes 30724
  189.0 222.7 %all-to-all-start.2 = ((bf16[320,8,1728]{2,0,1:T(8,128)(2,1)}), bf16[320,8,1728]{2,0,1:T(8,128)(2,1)}, u32[]{:S(2)}, u32[]{:S(2)}) async-start(bf16[320,8,1728]{2,0,1:T(8,128)(2,1)} %copy.68), calls=%async_computation.2 | async-start | bytes 18350080 | tf_op jit(solution)/shard_map/all_to_all | solution.py:117
  194.0 212.6 %all-reduce.2.cloned.1.call-start = ((), (), s32[]{:S(2)}) async-start(), calls=%async_computation.4 | async-start | bytes 5242880 | tf_op jit(solution)/shard_map/psum | solution.py:213
  255.1 271.7 %reduce-scatter.4.cloned.1.call-start = ((), (), s32[]{:S(2)}) async-start(), calls=%async_computation.7 | async-start | bytes 2949120
  434.3 14.4 %copy-start.4 = (f32[2560]{0:T(1024)S(1)}, f32[2560]{0:T(1024)}, u32[]{:S(2)}) copy-start(f32[2560]{0:T(1024)} %param.18) | copy-start | bytes 30724
Sparse Core Ops, SparseCore 0:
  10.9 57.9 all-gather.4
  71.3 91.7 all-gather.6
  255.2 151.3 all-reduce.1
  465.1 61.6 reduce-scatter.3
where the time goes:
time: 543 us; the launch traced here: 536 us
  waiting for transfers between devices  301 us (55%)
  local copies, waits for them, and re-layouts  97.1 us (18%)
  matrix products  58.8 us (11%)
  other arithmetic  46.1 us (8%)
  starting transfers between devices  18.5 us (3%)
  between operations  13.6 us (3%)
    psum x1, waiting for transfers between devices, shards(): lax.psum(projected_out.astype(jnp.bfloat16), 'kv').astype(jnp.float32)  151 us
    unnamed x5, waiting for transfers between devices  61.9 us
    all_gather x1, waiting for transfers between devices, shards(): lax.all_gather(merged_attn, 'blk', axis=0, tiled=True)  41.5 us
    all_to_all x3, local copies, waits for them, and re-layouts, shards(): lax.all_to_all(collected[1], 'kv', split_axis=1, concat_axis=0, tiled=True)  38 us
    all_to_all x1, waiting for transfers between devices, shards(): lax.all_to_all(collected[0], 'kv', split_axis=1, concat_axis=0, tiled=True)  29.5 us
    reshape x2, local copies, waits for them, and re-layouts, restack(): return jnp.transpose(ordered, (1, 0, 2, 3)).reshape(-1, columns)  19.9 us
    dot_general x8, matrix products, prefix_step(): jnp.einsum('gnqst,sgdt->gnqd', weights, value_part, preferred_element_typ...  18.6 us
    all_gather x1, waiting for transfers between devices, shards(): lax.all_gather(merged_mlp, 'blk', axis=0, tiled=True)  16.6 us
  transfers between devices with their start and end apart: 7, of which 5 were waited for; matrix products, arithmetic and copies ran while one was open for 21% of the time, Pallas kernels for 0%

commit v1 on v0

--- a/solution.py
+++ b/solution.py
@@ -14,6 +14,11 @@
 FLOOR_SCORE = -1e30
 EPSILON = 1e-05
 ROPE_BASE = 10000.0
+
+
+def summed_here(shard, mesh_axis):
+    pieces = lax.all_gather(shard, mesh_axis)
+    return jnp.sum(pieces, axis=0)
 
 
 def rms_scale(row_data, gain_vec):
@@ -210,7 +215,7 @@
         .astype(jnp.bfloat16)
     )
     projected_out = jnp.dot(attended, w_out, preferred_element_type=jnp.float32)
-    summed = lax.psum(projected_out.astype(jnp.bfloat16), "kv").astype(jnp.float32)
+    summed = summed_here(projected_out.astype(jnp.bfloat16), "kv").astype(jnp.float32)
     middle = (tokens.astype(jnp.float32) + summed).astype(jnp.bfloat16)
     normed_mid = rms_scale(middle, mlp_gain)
     paired = jnp.dot(normed_mid, w_pair, preferred_element_type=jnp.float32)

time: 543 us -> 836 us (1.54)
  blocking collectives: 0 us -> 207 us
  waiting for transfers between devices: 301 us -> 367 us
  local copies, waits for them, and re-layouts: 97.1 us -> 111 us
  other arithmetic: 46.1 us -> 58.1 us
    all_gather x0 -> x1, waiting for transfers between devices: none -> 234 us  [summed_here(): pieces = lax.all_gather(shard, mesh_axis)]
    all_to_all x0 -> x1, blocking collectives: none -> 207 us  [shards(): lax.all_to_all(collected[1], 'kv', split_axis=1, concat_axis=0, tiled=True)]
    psum x1 -> x0, waiting for transfers between devices: 151 us -> none  [shards(): lax.psum(projected_out.astype(jnp.bfloat16), 'kv').astype(jnp.float32)]
    reduce_scatter x0 -> x1, waiting for transfers between devices: none -> 63.4 us  [shards(): lax.psum_scatter(down_part.astype(jnp.bfloat16), 'kv', scatter_dimension=...]
    unnamed x5 -> x4, waiting for transfers between devices: 61.9 us -> 0.07 us
    all_gather x1, waiting for transfers between devices: 16.6 us -> 0.02 us  [shards(): lax.all_gather(merged_mlp, 'blk', axis=0, tiled=True)]
    reduce_sum x0 -> x1, other arithmetic: none -> 13.1 us  [summed_here(): return jnp.sum(pieces, axis=0)]
  transfers between devices with their start and end apart: 7 -> 6, of which waited for: 5 -> 4; matrix products, arithmetic and copies ran while one was open for 21% -> 19% of each run, Pallas kernels for 0% -> 0%
where the time goes in v1:
time: 836 us; the launch traced here: 829 us
  waiting for transfers between devices  367 us (44%)
  blocking collectives  207 us (25%)
  local copies, waits for them, and re-layouts  111 us (13%)
  other arithmetic  58.1 us (7%)
  matrix products  57.6 us (7%)
  between operations  13.7 us (2%)
  starting transfers between devices  13.4 us (2%)
    all_gather x1, waiting for transfers between devices, summed_here(): pieces = lax.all_gather(shard, mesh_axis)  234 us
    all_to_all x1, blocking collectives, shards(): lax.all_to_all(collected[1], 'kv', split_axis=1, concat_axis=0, tiled=True)  207 us
    reduce_scatter x1, waiting for transfers between devices, shards(): lax.psum_scatter(down_part.astype(jnp.bfloat16), 'kv', scatter_dimension=...  63.4 us
    all_gather x1, waiting for transfers between devices, shards(): lax.all_gather(merged_attn, 'blk', axis=0, tiled=True)  40.8 us
    all_to_all x3, local copies, waits for them, and re-layouts, shards(): lax.all_to_all(collected[1], 'kv', split_axis=1, concat_axis=0, tiled=True)  37.8 us
    all_to_all x1, waiting for transfers between devices, shards(): lax.all_to_all(collected[0], 'kv', split_axis=1, concat_axis=0, tiled=True)  29.5 us
    reshape x2, local copies, waits for them, and re-layouts, restack(): return jnp.transpose(ordered, (1, 0, 2, 3)).reshape(-1, columns)  19.7 us
    dot_general x8, matrix products, prefix_step(): jnp.einsum('gnqst,sgdt->gnqd', weights, value_part, preferred_element_typ...  18.6 us
  transfers between devices with their start and end apart: 6, of which 4 were waited for; matrix products, arithmetic and copies ran while one was open for 19% of the time, Pallas kernels for 0%

profile of v1, /device:TPU:1, one launch (start us, length us, event | category | flops | bytes accessed | tf_op | source)
XLA Modules:
  0.0 828.9 jit_solution(13409117487098557881)
XLA Ops:
  16.2 8.6 %all-to-all-start.1 = ((bf16[2,32,1,80,128]{4,3,0,2,1:T(8,128)(2,1)}), bf16[2,32,1,80,128]{4,3,0,2,1:T(8,128)(2,1)S(1)}, u32[]{:S(2)}, u32[]{:S(2)}) async-start(bf16[2,32,1,80,128]{4,3,0,2,1:T(8,128)(2,1)} %fusion.67), calls=%async_computation.1 | async-start | bytes 2621440 | tf_op jit(solution)/shard_map/all_to_all | solution.py:177
  32.4 40.8 %all-gather.9.cloned.1.call-done = bf16[16,20,3840]{2,1,0:T(8,128)(2,1)} async-done(((bf16[1,20,3840]{2,1,0:T(8,128)(2,1)}), bf16[16,20,3840]{2,1,0:T(8,128)(2,1)}) %all-gather.9.cloned.1.call-update) | async-done | bytes 2457616 | tf_op jit(solution)/shard_map/all_gather | solution.py:117
  73.2 6.5 all_to_all.27
  79.7 4.1 copy.47
  83.8 4.4 all-to-all-start
  89.8 4.4 copy.46
  101.0 29.5 %all-to-all-done = bf16[320,8,480]{2,0,1:T(8,128)(2,1)} async-done(((bf16[320,8,480]{2,0,1:T(8,128)(2,1)}), bf16[320,8,480]{2,0,1:T(8,128)(2,1)}, u32[]{:S(2)}, u32[]{:S(2)}) %all-to-all-start) | async-done | bytes 2457632 | tf_op jit(solution)/shard_map/all_to_all | solution.py:121
  130.5 3.2 copy.48
  136.5 5.5 reshape.470
  142.0 4.2 fusion.54
  151.0 63.4 %while.16 = (s32[]{:T(128)}, f32[1,4,512]{2,1,0:T(4,128)S(1)}, f32[1,4,512]{2,1,0:T(4,128)S(1)}, f32[1,4,512,80]{2,3,1,0:T(8,128)}, pred[8,4]{1,0:T(8,128)(4,1)S...) while((s32[]{:T(128)}, f32[1,4,512]{2,1,0:T(4,128)S(1)}, ...), condition=%wide.region_14.15_spmd.clone.clone, body=%wide.region_11.14_spmd.clone.clone.sunk | while | flops 351253504 | bytes 20843776 | solution.py:209
  218.7 16.5 %all_to_all.31 = bf16[320,8,1728]{2,1,0:T(8,128)(2,1)} reshape(bf16[16,20,13824]{2,1,0:T(8,128)(2,1)} %all-gather.11.cloned.1.call-done) | data formatting | bytes 17694720 | tf_op jit(solution)/shard_map/all_to_all | solution.py:122
  235.2 9.0 %copy.54 = bf16[320,8,1728]{2,0,1:T(8,128)(2,1)} copy(bf16[320,8,1728]{2,1,0:T(8,128)(2,1)} %all_to_all.31) | data formatting | bytes 17694720 | tf_op jit(solution)/shard_map/all_to_all | solution.py:122
  244.3 207.0 %all_to_all.37 = bf16[320,8,1728]{2,0,1:T(8,128)(2,1)} all-to-all(bf16[320,8,1728]{2,0,1:T(8,128)(2,1)} %copy.54), channel_id=1, replica_groups=mesh['blk'=16,'kv'=8] {'kv'}, dimensions={1} | all-to-all | bytes 17694720 | tf_op jit(solution)/shard_map/all_to_all | solution.py:122
  451.3 12.3 %copy.55 = bf16[320,8,1728]{2,1,0:T(8,128)(2,1)} copy(bf16[320,8,1728]{2,0,1:T(8,128)(2,1)} %all_to_all.37) | data formatting | bytes 17694720 | tf_op jit(solution)/shard_map/all_to_all | solution.py:122
  463.6 10.4 %copy.56 = bf16[16,8,20,1728]{3,2,1,0:T(8,128)(2,1)} copy(bf16[16,8,20,1728]{3,1,2,0:T(8,128)(2,1)} %bitcast.200) | data formatting | bytes 17694720 | tf_op jit(solution)/shard_map/transpose | solution.py:91
  474.0 14.2 %reshape.479 = bf16[2560,1728]{1,0:T(8,128)(2,1)} reshape(bf16[16,8,20,1728]{3,2,1,0:T(8,128)(2,1)} %copy.56) | data formatting | bytes 17694720 | tf_op jit(solution)/shard_map/reshape | solution.py:91
  488.2 233.7 %all-gather.7.cloned.1.call-done = bf16[4096,2560]{1,0:T(8,128)(2,1)} async-done(((bf16[512,2560]{1,0:T(8,128)(2,1)}), bf16[4096,2560]{1,0:T(8,128)(2,1)}) %all-gather.7.cloned.1.call-update) | async-done | bytes 20971536 | tf_op jit(solution)/shard_map/all_gather | solution.py:20
  721.9 13.1 %reduce_sum.101 = bf16[512,2560]{1,0:T(8,128)(2,1)} reduce(bf16[8,512,2560]{2,1,0:T(8,128)(2,1)} %bitcast.201, bf16[]{:T(256)} %constant.118.clone.1), dimensions={0}, to_apply=%region_15.16 | reduce | flops 9175040 | bytes 23592962 | tf_op jit(solution)/shard_map/reduce_sum | solution.py:21
  735.0 4.4 copy.53
  739.4 3.7 fusion.44
  743.2 9.2 %fusion.56 = f32[512,1728]{0,1:T(8,128)S(1)} fusion(bf16[2560,1728]{1,0:T(8,128)(2,1)} %reshape.479, bf16[512,2560]{0,1:T(8,128)(2,1)S(1)} %get-tuple-element.174, f32[2560]{0:T(1024)S(1)} %copy-done.7, f32[512]{0:T(512)S(1)} %add_rsqrt_fusion), kind=kOutput, calls=%fused_computation.67 | convolution fusion | flops 4535091200 | bytes 15020032 | tf_op jit(solution)/shard_map/dot_general | solution.py:221
  752.4 4.4 convolution_convert_fusion
  756.9 63.4 %reduce-scatter.2.cloned.1.call-done = bf16[512,320]{0,1:T(8,128)(2,1)} async-done(((bf16[512,2560]{0,1:T(8,128)(2,1)}), bf16[512,320]{0,1:T(8,128)(2,1)}) %reduce-scatter.2.cloned.1.call-update) | async-done | bytes 327696 | tf_op jit(solution)/shard_map/reduce_scatter | solution.py:225
  (218 shorter events, 101.5 us)
Async XLA Ops:
  6.5 209.0 %copy-start = (bf16[320,2560]{1,0:T(8,128)(2,1)S(1)}, bf16[320,2560]{1,0:T(8,128)(2,1)}, u32[]{:S(2)}) copy-start(bf16[320,2560]{1,0:T(8,128)(2,1)} %param.24) | copy-start | bytes 4915204
  6.5 66.6 %all-gather.9.cloned.1.call-start = ((), (), s32[]{:S(2)}) async-start(), calls=%async_computation.6 | async-start | bytes 3133440 | tf_op jit(solution)/shard_map/all_gather | solution.py:117
  16.2 16.1 %copy-start.5 = (s32[128]{0:T(128)S(1)}, s32[128]{0:T(128)}, u32[]{:S(2)}) copy-start(s32[128]{0:T(128)} %param.27) | copy-start | bytes 1540
  16.2 67.6 %all-to-all-start.1 = ((bf16[2,32,1,80,128]{4,3,0,2,1:T(8,128)(2,1)}), bf16[2,32,1,80,128]{4,3,0,2,1:T(8,128)(2,1)S(1)}, u32[]{:S(2)}, u32[]{:S(2)}) async-start(bf16[2,32,1,80,128]{4,3,0,2,1:T(8,128)(2,1)} %fusion.67), calls=%async_computation.1 | async-start | bytes 2621440 | tf_op jit(solution)/shard_map/all_to_all | solution.py:177
  24.8 194.0 %all-gather.11.cloned.1.call-start = ((), (), s32[]{:S(2)}) async-start(), calls=%async_computation.7 | async-start | bytes 11280384 | tf_op jit(solution)/shard_map/all_gather | solution.py:118
  79.7 8.9 %copy-start.8 = (s32[16]{0:T(128)S(1)}, s32[16]{0:T(128)}, u32[]{:S(2)}) copy-start(s32[16]{0:T(128)} %param.28) | copy-start | bytes 196
  79.7 9.4 %copy-start.9 = (s32[16]{0:T(128)S(1)}, s32[16]{0:T(128)}, u32[]{:S(2)}) copy-start(s32[16]{0:T(128)} %param.29) | copy-start | bytes 196
  83.8 46.7 %all-to-all-start = ((bf16[320,8,480]{2,0,1:T(8,128)(2,1)}), bf16[320,8,480]{2,0,1:T(8,128)(2,1)}, u32[]{:S(2)}, u32[]{:S(2)}) async-start(bf16[320,8,480]{2,0,1:T(8,128)(2,1)} %copy.47), calls=%async_computation | async-start | bytes 5242880 | tf_op jit(solution)/shard_map/all_to_all | solution.py:121
  88.2 633.7 %all-gather.7.cloned.1.call-start = ((), (), s32[]{:S(2)}) async-start(), calls=%async_computation.5 | async-start | bytes 23592960 | tf_op jit(solution)/shard_map/all_gather | solution.py:20
  136.5 5.5 copy-start.6
  153.2 3.0 copy-start.3
  161.1 3.0 copy-start.3
  169.0 3.0 copy-start.3
  176.8 3.0 copy-start.3
  184.7 3.0 copy-start.3
  192.5 3.0 copy-start.3
  200.4 3.0 copy-start.3
  208.2 3.0 copy-start.3
  218.7 601.6 %reduce-scatter.2.cloned.1.call-start = ((), (), s32[]{:S(2)}) async-start(), calls=%async_computation.4 | async-start | bytes 2949120 | tf_op jit(solution)/shard_map/reduce_scatter | solution.py:225
  739.4 3.8 copy-start.7
  739.4 13.0 %slice-start = ((s8[4423680]{0:T(1024)(128)(4,1)}), s8[4194304]{0:T(1024)(128)(4,1)S(1)}, s32[]{:S(2)}) async-start(s8[4423680]{0:T(1024)(128)(4,1)} %bitcast.213), calls=%async_computation.8 | async-start | bytes 8388608
  743.1 9.2 %copy-start.2 = (bf16[512,2560]{0,1:T(8,128)(2,1)}, bf16[512,2560]{0,1:T(8,128)(2,1)S(1)}, u32[]{:S(2)}) copy-start(bf16[512,2560]{0,1:T(8,128)(2,1)S(1)} %get-tuple-element.174) | copy-start | bytes 7864324
  743.1 9.2 %slice-start.1 = ((s8[4423680]{0:T(1024)(128)(4,1)}), s8[229376]{0:T(1024)(128)(4,1)S(1)}, s32[]{:S(2)}) async-start(s8[4423680]{0:T(1024)(128)(4,1)} %bitcast.213), calls=%async_computation.9 | async-start | bytes 458752
  752.4 69.8 %copy-start.1 = (bf16[320,2560]{1,0:T(8,128)(2,1)S(1)}, bf16[320,2560]{1,0:T(8,128)(2,1)}, u32[]{:S(2)}) copy-start(bf16[320,2560]{1,0:T(8,128)(2,1)} %param.24) | copy-start | bytes 4915204
  (8 other events, 6.8 us)
Sparse Core Ops, SparseCore 0:
  10.9 62.2 all-gather.8
  75.6 91.7 all-gather.10
  218.8 503.0 all-gather.6
  757.0 63.2 reduce-scatter.1
